TPU v7x, 256 devices: a whole 4x4x8 slice. The times are simulated.
256 devices in a mesh: dp: 16 (over z, core), tensor: 16 (over x, y).
Axes of the slice: x: 4, y: 4, z: 8, core: 2. Of those that a mesh axis runs over, the one named last changes fastest.
Arguments:
- queries: bfloat16 [2048, 8192], P('dp', 'tensor'), parts along dimension 0
- tree_states: bfloat16 [2048, 2048], P(('dp', 'tensor')), parts along dimension 0, may hold values from -6 to 6
- cache_codes: bfloat16 [5120, 8, 2, 64, 128], P(('dp', 'tensor')), parts along dimension 0, may hold values from 0 to 255, as said below
- cache_scales: float32 [5120, 8, 2, 128], P(('dp', 'tensor')), parts along dimension 0, may hold values from 0.3 to 3
- bit_widths: int32 [128], P('dp'), parts along dimension 0, may hold values from 2 to 8, as said below
- page_table: int32 [64, 80], P('dp'), parts along dimension 0, may hold values from 0 to 19, as said below
- lengths: int32 [64], P('dp'), parts along dimension 0, may hold values from 1 to 5120, as said below
- parents: int32 [64, 32], P('dp'), parts along dimension 0, may hold values from 0 to 30, as said below
- tree_mask: int32 [64, 32, 32], P('dp'), parts along dimension 0, may hold values from 0 to 1, as said below
- output_weight: bfloat16 [8192, 8192], P('tensor'), may hold values from -0.09375 to 0.09375
- residual: bfloat16 [2048, 8192], P('dp', 'tensor'), parts along dimension 0
- norm_gain: bfloat16 [8192], P('tensor'), may hold values from 0.099609375 to 1.8984375
- draft_weight: bfloat16 [8192, 2048], P('tensor'), may hold values from -0.09375 to 0.09375
Outputs:
- feature: bfloat16 [2048, 8192], P('dp', 'tensor'), parts along dimension 0
- draft_projection: bfloat16 [2048, 2048], P('dp', 'tensor'), parts along dimension 0
There are 16 independent parts, one for each index of `dp`. A program takes and returns all parts, laid end to end along the dimension named above; an argument that names none is the same for every part. Nothing has to cross between parts.
Inputs may be any that keep to these rules, and one draw needn't show every extreme that they name: `bit_widths`: every head holds 2, 4 or 8 bits. `cache_codes`: on KV head g every entry is a whole number from 0 to 2 to the power bit_widths[g], minus 1. `page_table`: for each c, the entries of columns c * 5 to (c + 1) * 5 - 1 over all requests form a permutation of 0 to 19: slots in the pool of tensor index c. `lengths`: some request of every part has exactly 5120 positions. parents[r, 0] = 0; for i > 0 the parent is below i, in node i's own block of 8 nodes, or in the first block when i is the first node of its block. tree_mask[r, i, j] = 1 exactly when j is i or an ancestor of i under parents.
All inputs are finite; a program needn't handle non-finite values.
Results may differ from a plain program's by a relative error of at most 0.012.
Values may be sent and summed in bfloat16 or wider, within the bound.
No kernel may reach another device: no remote copies, remote signals or barrier semaphores. Data moves between devices by JAX's collectives and lax.ppermute only.
A program may use at most 128 MiB of HBM per device.

v0:
```python
import math

import jax
import jax.numpy as jnp
from jax import lax
from jax.sharding import PartitionSpec as P

D = 8192
HQ = 64
KVH = 8
HD = 128
NODES = 32
PAGE = 64
PAGES_DEV = 5
REQS = 4
ROWS = 128


masked_score = -1e30
epsilon = 1e-05


def dequantize(cache_codes, cache_scales, bit_widths):
    levels = jnp.exp2(bit_widths.astype(jnp.float32))[None, :, None, None, None]
    drawn = cache_codes.astype(jnp.float32)
    scaled = cache_scales[:, :, :, None, :]
    return (scaled * (2.0 * drawn - levels + 1.0) / levels).astype(jnp.bfloat16)


def block_partial(request_query, key_rows, value_rows, in_range):
    scores = jnp.einsum(
        "nkgd,ktd->nkgt", request_query, key_rows, preferred_element_type=jnp.float32
    ) / math.sqrt(HD)
    live = in_range[None, None, None, :]
    scores = jnp.where(live, scores, masked_score)
    block_max = jnp.max(scores, axis=-1)
    weights = jnp.where(live, jnp.exp(scores - block_max[..., None]), 0.0)
    block_sum = jnp.sum(weights, axis=-1)
    block_out = jnp.einsum(
        "nkgt,ktd->nkgd",
        weights.astype(jnp.bfloat16),
        value_rows,
        preferred_element_type=jnp.float32,
    )
    block_out = block_out / jnp.where(block_sum > 0, block_sum, 1.0)[..., None]
    return (block_max, block_sum, block_out.astype(jnp.bfloat16))


def page_rows(chosen, heads_held, block_span):
    key_rows = chosen[:, :, 0].transpose(1, 0, 2, 3).reshape(heads_held, block_span, HD)
    value_rows = chosen[:, :, 1].transpose(1, 0, 2, 3).reshape(heads_held, block_span, HD)
    return (key_rows, value_rows)


def shards(
    queries,
    tree_states,
    cache_codes,
    cache_scales,
    bit_widths,
    page_table,
    lengths,
    parents,
    tree_mask,
    output_weight,
    residual,
    norm_gain,
    draft_weight,
):
    position = lax.axis_index("tensor")
    heads_dev = queries.shape[1] // HD
    groups = HQ // KVH
    block_span = PAGES_DEV * PAGE
    dequant = dequantize(cache_codes, cache_scales, bit_widths)
    every_query, tree_all = (
        lax.all_gather(queries, "tensor", axis=1, tiled=True),
        lax.all_gather(tree_states, "tensor", axis=0, tiled=True),
    )

    def one_request(request):
        request_query = lax.dynamic_slice_in_dim(every_query, request * NODES, NODES, 0).reshape(
            NODES, KVH, groups, HD
        )
        request_pages = lax.dynamic_index_in_dim(page_table, request, 0, keepdims=False)
        slot_ids = lax.dynamic_slice_in_dim(request_pages, position * PAGES_DEV, PAGES_DEV)
        key_rows, value_rows = page_rows(jnp.take(dequant, slot_ids, axis=0), KVH, block_span)
        positions = position * block_span + jnp.arange(block_span, dtype=jnp.int32)
        block_max, block_sum, block_out = block_partial(
            request_query, key_rows, value_rows, positions < lengths[request]
        )
        return (
            block_out.reshape(NODES, HQ * HD),
            block_max.reshape(NODES, HQ),
            block_sum.reshape(NODES, HQ),
        )

    partial_out, maxima, partial_sum = lax.map(one_request, jnp.arange(REQS, dtype=jnp.int32))
    partial_out = partial_out.reshape(ROWS, HQ * HD)
    maxima = maxima.reshape(ROWS, HQ)
    partial_sum = partial_sum.reshape(ROWS, HQ)
    row_max = lax.pmax(maxima, "tensor")
    weight = jnp.exp(maxima - row_max) * partial_sum
    weighted = (weight[..., None] * partial_out.astype(jnp.float32).reshape(ROWS, HQ, HD)).reshape(
        ROWS, HQ * HD
    )
    numerator, denominator = (
        lax.psum_scatter(weighted, "tensor", scatter_dimension=1, tiled=True),
        lax.psum_scatter(weight, "tensor", scatter_dimension=1, tiled=True),
    )
    context_max = lax.dynamic_slice_in_dim(row_max, position * heads_dev, heads_dev, 1)
    context_max = context_max.reshape(REQS, NODES, heads_dev)
    numerator = numerator.reshape(REQS, NODES, heads_dev, HD)
    denominator = denominator.reshape(REQS, NODES, heads_dev)
    tree_keys = tree_all[:, : KVH * HD].reshape(ROWS, KVH, HD)
    tree_values = tree_all[:, KVH * HD :].reshape(ROWS, KVH, HD)
    head_ids = (position * heads_dev + jnp.arange(heads_dev, dtype=jnp.int32)) // groups
    own_keys = jnp.take(tree_keys, head_ids, axis=1).reshape(REQS, NODES, heads_dev, HD)
    own_values = jnp.take(tree_values, head_ids, axis=1).reshape(REQS, NODES, heads_dev, HD)
    local_query = queries.reshape(REQS, NODES, heads_dev, HD)
    allowed = (tree_mask > 0)[:, :, None, :]
    tree_scores = jnp.einsum(
        "rnhd,rjhd->rnhj", local_query, own_keys, preferred_element_type=jnp.float32
    ) / math.sqrt(HD)
    tree_scores = jnp.where(allowed, tree_scores, masked_score)
    overall = jnp.maximum(context_max, jnp.max(tree_scores, axis=-1))
    rescale = jnp.exp(context_max - overall)
    tree_weights = jnp.where(allowed, jnp.exp(tree_scores - overall[..., None]), 0.0)
    total_numerator = numerator * rescale[..., None] + jnp.einsum(
        "rnhj,rjhd->rnhd",
        tree_weights.astype(jnp.bfloat16),
        own_values,
        preferred_element_type=jnp.float32,
    )
    total_denominator = denominator * rescale + jnp.sum(tree_weights, axis=-1)
    attended = (
        (total_numerator / total_denominator[..., None])
        .astype(jnp.bfloat16)
        .reshape(ROWS, heads_dev * HD)
    )
    projected = lax.psum_scatter(
        jnp.dot(attended, output_weight, preferred_element_type=jnp.float32),
        "tensor",
        scatter_dimension=1,
        tiled=True,
    )
    feature = (residual.astype(jnp.float32) + projected).astype(jnp.bfloat16)
    squares = lax.psum(jnp.sum(jnp.square(feature.astype(jnp.float32)), axis=1), "tensor")
    inverse = lax.rsqrt(squares / D + epsilon)
    normed = (
        feature.astype(jnp.float32) * inverse[:, None] * norm_gain.astype(jnp.float32)[None, :]
    ).astype(jnp.bfloat16)
    row_ids = (jnp.arange(REQS, dtype=jnp.int32)[:, None] * NODES + parents).reshape(ROWS)
    chosen_rows = jnp.take(normed, row_ids, axis=0)
    drafted = lax.psum_scatter(
        jnp.dot(chosen_rows, draft_weight, preferred_element_type=jnp.float32),
        "tensor",
        scatter_dimension=1,
        tiled=True,
    )
    return (feature, drafted.astype(jnp.bfloat16))


def solution(mesh):
    placed = (
        P("dp", "tensor"),
        P(("dp", "tensor"), None),
        P(("dp", "tensor"), None, None, None, None),
        P(("dp", "tensor"), None, None, None),
        P("dp"),
        P("dp", None),
        P("dp"),
        P("dp", None),
        P("dp", None, None),
        P("tensor", None),
        P("dp", "tensor"),
        P("tensor"),
        P("tensor", None),
    )
    return jax.shard_map(
        shards,
        mesh=mesh,
        in_specs=placed,
        out_specs=(P("dp", "tensor"), P("dp", "tensor")),
        check_vma=False,
    )
```

profile of v0, /device:TPU:2, one launch (start us, length us, event | category | flops | bytes accessed | tf_op | source)
XLA Modules:
  0.0 531.3 jit_solution(6231793858506092336)
XLA Ops:
  8.7 7.5 %divide_convert_fusion.1 = bf16[20,8,2,64,128]{4,3,2,1,0:T(8,128)(2,1)} fusion(bf16[20,8,2,64,128]{4,3,2,1,0:T(8,128)(2,1)} %param.19, f32[8]{0:T(128)S(1)} %multiply_exponential_fusion, f32[20,8,2,128]{3,2,1,0:T(2,128)} %param.20), kind=kLoop, calls=%fused_computation.39 | loop fusion | flops 18350080 | bytes 10649632 | tf_op jit(solution)/shard_map/convert_element_type | solution.py:27
  16.2 48.9 %all-gather.2.cloned.1.call-done = bf16[128,8192]{1,0:T(8,128)(2,1)} async-done(((bf16[128,512]{1,0:T(8,128)(2,1)}), bf16[128,8192]{1,0:T(8,128)(2,1)}) %all-gather.2.cloned.1.call-update) | async-done | bytes 2097168 | tf_op jit(solution)/shard_map/all_gather | solution.py:76
  65.1 74.1 %while.17 = (s32[]{:T(128)}, bf16[4,32,8192]{2,1,0:T(8,128)(2,1)}, f32[4,32,64]{2,1,0:T(8,128)S(1)}, f32[4,32,64]{2,1,0:T(8,128)}, s32[4]{0:T(128)S(1)}, /*index...) while((s32[]{:T(128)}, bf16[4,32,8192]{2,1,0:T(8,128)(2,1)}, ...), condition=%wide.region_3.4_spmd, body=%wide.region_0.3_spmd.sunk | while | flops 345245376 | bytes 36600504 | solution.py:97
  67.9 3.3 gather_fusion
  76.0 1.6 copy-done.1
  79.5 2.8 divide_convert_fusion.3
  86.5 3.3 gather_fusion
  94.5 1.6 copy-done.1
  98.0 2.8 divide_convert_fusion.3
  105.0 3.3 gather_fusion
  113.0 1.6 copy-done.1
  116.6 2.8 divide_convert_fusion.3
  123.5 3.3 gather_fusion
  131.6 1.6 copy-done.1
  135.1 2.8 divide_convert_fusion.3
  139.2 66.4 %pmax.7 = f32[128,64]{1,0:T(8,128)S(1)} all-reduce(f32[128,64]{1,0:T(8,128)S(1)} %bitcast.153), channel_id=1, replica_groups=mesh['dp'=16,'tensor'=16] {'tensor'}, use_global_device_ids=true, to_apply=%region_4.5 | all-reduce | flops 8192 | bytes 65536 | tf_op jit(solution)/shard_map/pmax | solution.py:101
  207.8 5.7 %bitcast_multiply_fusion = f32[128,8192]{1,0:T(8,128)} fusion(f32[16,8,64,128]{3,2,1,0:T(8,128)S(1)} %bitcast.144, bf16[4,32,8192]{2,1,0:T(8,128)(2,1)S(1)} %copy-done.2), kind=kLoop, calls=%fused_computation.40 | loop fusion | flops 2097152 | bytes 10485760 | tf_op jit(solution)/shard_map/mul | solution.py:103
  214.5 28.0 %all_gather.7 = bf16[128,2048]{1,0:T(8,128)(2,1)S(1)} all-gather(bf16[8,2048]{1,0:T(8,128)(2,1)S(1)} %copy-done.7), channel_id=1, replica_groups=mesh['dp'=16,'tensor'=16] {'tensor'}, dimensions={0}, use_global_device_ids=true | all-gather | bytes 557056 | tf_op jit(solution)/shard_map/all_gather | solution.py:77
  246.4 65.4 %all-reduce = f32[128,64]{1,0:T(8,128)S(1)} all-reduce(f32[128,64]{1,0:T(8,128)S(1)} %bitcast_multiply_fusion.1), channel_id=3, replica_groups=mesh['dp'=16,'tensor'=16] {'tensor'}, use_global_device_ids=true, to_apply=%region_7.9.clone | all-reduce | flops 8192 | bytes 65536
  313.5 6.6 %fusion.34 = f32[128,8192]{1,0:T(8,128)} fusion(bf16[512,8192]{1,0:T(8,128)(2,1)} %param.26, bf16[16,8,4,128]{3,2,1,0:T(4,128)(2,1)S(1)} %bitcast.150), kind=kOutput, calls=%fused_computation.58 | convolution fusion | flops 1073741824 | bytes 12713984 | tf_op jit(solution)/shard_map/dot_general | solution.py:141
  321.0 84.9 %reduce-scatter.7.cloned.1.call-done = f32[128,512]{1,0:T(8,128)} async-done(((f32[128,8192]{1,0:T(8,128)}), f32[128,512]{1,0:T(8,128)}) %reduce-scatter.7.cloned.1.call-update) | async-done | bytes 262160 | tf_op jit(solution)/shard_map/reduce_scatter | solution.py:140
  407.0 33.3 %psum.7 = f32[128]{0:T(128)S(1)} all-reduce(f32[128]{0:T(128)S(1)} %get-tuple-element.207), channel_id=1, replica_groups=mesh['dp'=16,'tensor'=16] {'tensor'}, use_global_device_ids=true, to_apply=%region_11.13 | all-reduce | flops 128 | bytes 1024 | tf_op jit(solution)/shard_map/psum | solution.py:147
  441.3 1.5 fusion.40
  442.8 80.5 %reduce-scatter.9.cloned.1.call-done = f32[128,128]{1,0:T(8,128)} async-done(((f32[128,2048]{1,0:T(8,128)}), f32[128,128]{1,0:T(8,128)}) %reduce-scatter.9.cloned.1.call-update) | async-done | bytes 65552 | tf_op jit(solution)/shard_map/reduce_scatter | solution.py:154
  (167 shorter events, 45.3 us)
Async XLA Ops:
  7.2 434.1 %copy-start = (bf16[512,2048]{1,0:T(8,128)(2,1)S(1)}, bf16[512,2048]{1,0:T(8,128)(2,1)}, u32[]{:S(2)}) copy-start(bf16[512,2048]{1,0:T(8,128)(2,1)} %param.29) | copy-start | bytes 6291460
  7.2 57.9 %all-gather.2.cloned.1.call-start = ((), (), s32[]{:S(2)}) async-start(), calls=%async_computation.3 | async-start | bytes 2228224 | tf_op jit(solution)/shard_map/all_gather | solution.py:76
  7.9 304.2 %reduce-scatter.5.cloned.1.call-start = ((), (), s32[]{:S(2)}) async-start(), calls=%async_computation.4 | async-start | bytes 4456448 | tf_op jit(solution)/shard_map/reduce_scatter | solution.py:107
  8.7 56.4 %copy-start.8 = (s32[4,80]{1,0:T(4,128)S(1)}, s32[4,80]{1,0:T(4,128)}, u32[]{:S(2)}) copy-start(s32[4,80]{1,0:T(4,128)} %param.22) | copy-start | bytes 3844
  8.7 56.4 %copy-start.11 = (s32[4]{0:T(128)S(1)}, s32[4]{0:T(128)}, u32[]{:S(2)}) copy-start(s32[4]{0:T(128)} %param.23) | copy-start | bytes 52
  75.9 1.7 copy-start.1
  94.5 1.7 copy-start.1
  113.0 1.7 copy-start.1
  131.5 1.7 copy-start.1
  205.6 2.2 copy-start.2
  213.5 0.9 copy-start.4
  213.5 0.9 copy-start.7
  213.5 30.9 %copy-start.6 = (s32[4,32,32]{2,1,0:T(8,128)S(1)}, s32[4,32,32]{2,1,0:T(8,128)}, u32[]{:S(2)}) copy-start(s32[4,32,32]{2,1,0:T(8,128)} %param.25) | copy-start | bytes 49156
  213.5 31.1 %copy-start.12 = (u32[256]{0:T(256)S(1)}, u32[256]{0:T(256)}, u32[]{:S(2)}) copy-start(u32[256]{0:T(256)} %constant.235) | copy-start | bytes 3076
  213.5 192.4 %reduce-scatter.7.cloned.1.call-start = ((), (), s32[]{:S(2)}) async-start(), calls=%async_computation.5 | async-start | bytes 4456448 | tf_op jit(solution)/shard_map/reduce_scatter | solution.py:140
  320.1 0.7 copy-start.9
  320.1 0.9 copy-start.10
  320.1 85.9 %copy-start.5 = (bf16[128,512]{1,0:T(8,128)(2,1)S(1)}, bf16[128,512]{1,0:T(8,128)(2,1)}, u32[]{:S(2)}) copy-start(bf16[128,512]{1,0:T(8,128)(2,1)} %param.27) | copy-start | bytes 393220
  320.1 203.2 %reduce-scatter.9.cloned.1.call-start = ((), (), s32[]{:S(2)}) async-start(), calls=%async_computation.6 | async-start | bytes 1114112 | tf_op jit(solution)/shard_map/reduce_scatter | solution.py:154
  407.0 117.8 %copy-start.3 = (bf16[128,512]{1,0:T(8,128)(2,1)}, bf16[128,512]{1,0:T(8,128)(2,1)S(1)}, u32[]{:S(2)}) copy-start(bf16[128,512]{1,0:T(8,128)(2,1)S(1)} %get-tuple-element.208) | copy-start | bytes 393220
Sparse Core Ops, SparseCore 0:
  10.4 54.6 all-gather.1
  213.6 86.2 reduce-scatter.4
  320.2 85.6 reduce-scatter.6
  442.9 80.3 reduce-scatter.8
where the time goes:
time: 532 us; the launch traced here: 531 us
  waiting for transfers between devices  215 us (40%)
  blocking collectives  193 us (36%)
  local copies, waits for them, and re-layouts  46.4 us (9%)
  other arithmetic  26.4 us (5%)
  matrix products  24 us (5%)
  between operations  14.7 us (3%)
  loops' own time  11.5 us (2%)
    reduce_scatter x1, waiting for transfers between devices, shards(): lax.psum_scatter(jnp.dot(attended, output_weight, preferred_element_type=...  84.9 us
    reduce_scatter x1, waiting for transfers between devices, shards(): lax.psum_scatter(jnp.dot(chosen_rows, draft_weight, preferred_element_typ...  80.5 us
    pmax x1, blocking collectives, shards(): row_max = lax.pmax(maxima, 'tensor')  66.4 us
    unnamed x1, blocking collectives  65.4 us
    all_gather x1, waiting for transfers between devices, shards(): lax.all_gather(queries, 'tensor', axis=1, tiled=True)  48.9 us
    psum x1, blocking collectives, shards(): lax.psum(jnp.sum(jnp.square(feature.astype(jnp.float32)), axis=1), 'tensor')  33.3 us
    all_gather x1, blocking collectives, shards(): lax.all_gather(tree_states, 'tensor', axis=0, tiled=True)  28 us
    gather x4, local copies, waits for them, and re-layouts, one_request(): jnp.take(dequant, slot_ids, axis=0)  13.1 us
  transfers between devices with their start and end apart: 4, of which 3 were waited for; matrix products, arithmetic and copies ran while one was open for 2% of the time, Pallas kernels for 0%

commit v1 on v0

v1 whole, which is shorter than its diff:
```python
import math

import jax
import jax.numpy as jnp
from jax import lax
from jax.experimental import pallas as pl
from jax.experimental.pallas import tpu as pltpu
from jax.sharding import PartitionSpec as P

D = 8192
HQ = 64
KVH = 8
HD = 128
NODES = 32
PAGE = 64
PAGES_DEV = 5
REQS = 4
ROWS = 128
N_TENSOR = 16
SPAN = PAGES_DEV * PAGE
GROUPS = HQ // KVH
HEADS = HQ // N_TENSOR
QCOLS = HEADS * HD

masked_score = -1e30
epsilon = 1e-05
SCALE = math.log2(math.e) / math.sqrt(HD)

OUT_ROWS = REQS * HD
LSE_AT = OUT_ROWS
TREE_AT = OUT_ROWS + 16
XROWS = OUT_ROWS + 32

bf16 = jnp.bfloat16
f32 = jnp.float32


def dot(a, b, dims):
    return lax.dot_general(a, b, (dims, ((), ())), preferred_element_type=f32)


def split3(x):
    hi = x.astype(bf16)
    rest = x - hi.astype(f32)
    mid = rest.astype(bf16)
    lo = (rest - mid.astype(f32)).astype(bf16)
    return hi, mid, lo


def dequant_body(table, place, bits, *refs):
    codes = refs[:PAGES_DEV]
    scales = refs[PAGES_DEV : 2 * PAGES_DEV]
    keys, values = refs[2 * PAGES_DEV :]
    for g in range(KVH):
        levels = lax.shift_left(jnp.int32(1), bits[g]).astype(f32)
        inverse = 1.0 / jnp.full((1, HD), levels, f32)
        parts = []
        for p in range(PAGES_DEV):
            scaled = scales[p][0, g] * inverse
            drawn = codes[p][0, g].astype(f32)
            centred = 2.0 * drawn - (levels - 1.0)
            keys[0, g, p * PAGE : (p + 1) * PAGE, :] = (centred[0] * scaled[0:1]).astype(bf16)
            parts.append(centred[1] * scaled[1:2])
        values[0, g] = jnp.concatenate(parts, axis=0).T.astype(bf16)


def dequantize(codes, scales, bits, table, place):
    def code_spec(p):
        return pl.BlockSpec(
            (1, KVH, 2, PAGE, HD),
            lambda r, table, place, bits: (table[r, place[0] * PAGES_DEV + p], 0, 0, 0, 0),
        )

    def scale_spec(p):
        return pl.BlockSpec(
            (1, KVH, 2, HD),
            lambda r, table, place, bits: (table[r, place[0] * PAGES_DEV + p], 0, 0, 0),
        )

    pages = range(PAGES_DEV)
    return pl.pallas_call(
        dequant_body,
        grid_spec=pltpu.PrefetchScalarGridSpec(
            num_scalar_prefetch=3,
            grid=(REQS,),
            in_specs=[code_spec(p) for p in pages] + [scale_spec(p) for p in pages],
            out_specs=[
                pl.BlockSpec((1, KVH, SPAN, HD), lambda r, *_: (r, 0, 0, 0)),
                pl.BlockSpec((1, KVH, HD, SPAN), lambda r, *_: (r, 0, 0, 0)),
            ],
        ),
        out_shape=[
            jax.ShapeDtypeStruct((REQS, KVH, SPAN, HD), bf16),
            jax.ShapeDtypeStruct((REQS, KVH, HD, SPAN), bf16),
        ],
        cost_estimate=pl.CostEstimate(
            flops=20_000_000, bytes_accessed=2 * codes.size * 2, transcendentals=0
        ),
        name="dequantize",
    )(table, place, bits, *([codes] * PAGES_DEV), *([scales] * PAGES_DEV))


def block_body(place, lengths, queries, keys, values, tree, out, lse):
    r = pl.program_id(0)
    live_count = lengths[r] - place[0] * SPAN
    live = lax.broadcasted_iota(jnp.int32, (SPAN, 1), 0) < live_count
    for g in range(KVH):
        query = jnp.concatenate(
            [
                queries[2 * g + h // HEADS, :, (h % HEADS) * HD : (h % HEADS + 1) * HD]
                for h in range(GROUPS)
            ],
            axis=0,
        )
        scores = dot(keys[0, g], query, ((1,), (1,)))
        scores = jnp.where(live, scores, masked_score)
        largest = jnp.max(scores, axis=0, keepdims=True)
        weights = jnp.exp2((scores - largest) * SCALE)
        total = jnp.sum(weights, axis=0, keepdims=True)
        mixed = dot(values[0, g], weights.astype(bf16), ((1,), (0,))) * (1.0 / total)
        mixed = mixed.astype(bf16)
        block_lse = jnp.where(live_count > 0, largest * SCALE + jnp.log2(total), masked_score)
        for half in range(2):
            lanes = slice(half * HD, (half + 1) * HD)
            out[2 * g + half, pl.ds(pl.multiple_of(r * HD, HD), HD), :] = mixed[:, lanes]
            lse[2 * g + half, pl.ds(r, 1), :] = block_lse[:, lanes]

    @pl.when(r == REQS - 1)
    def _():
        for t in range(N_TENSOR):
            pieces = split3(lse[t, 0:REQS, :])
            out[t, LSE_AT : LSE_AT + 16, :] = jnp.concatenate(
                [p.astype(f32) for p in pieces] + [jnp.zeros((4, HD), f32)], axis=0
            ).astype(bf16)
            g = t // 2
            out[t, TREE_AT : TREE_AT + 16, :] = jnp.concatenate(
                [
                    tree[:, g * HD : (g + 1) * HD].astype(f32),
                    tree[:, (KVH + g) * HD : (KVH + g + 1) * HD].astype(f32),
                ],
                axis=0,
            ).astype(bf16)


def block_partial(place, lengths, queries, keys, values, tree):
    return pl.pallas_call(
        block_body,
        grid_spec=pltpu.PrefetchScalarGridSpec(
            num_scalar_prefetch=2,
            grid=(REQS,),
            in_specs=[
                pl.BlockSpec((N_TENSOR, NODES, QCOLS), lambda r, *_: (0, r, 0)),
                pl.BlockSpec((1, KVH, SPAN, HD), lambda r, *_: (r, 0, 0, 0)),
                pl.BlockSpec((1, KVH, HD, SPAN), lambda r, *_: (r, 0, 0, 0)),
                pl.BlockSpec((8, 2 * KVH * HD), lambda r, *_: (0, 0)),
            ],
            out_specs=pl.BlockSpec((N_TENSOR, XROWS, HD), lambda r, *_: (0, 0, 0)),
            scratch_shapes=[pltpu.VMEM((N_TENSOR, 8, HD), f32)],
        ),
        out_shape=jax.ShapeDtypeStruct((N_TENSOR, XROWS, HD), bf16),
        cost_estimate=pl.CostEstimate(
            flops=1_400_000_000, bytes_accessed=10_000_000, transcendentals=2_600_000
        ),
        name="block_partial",
    )(place, lengths, queries, keys, values, tree)


WCOLS = 1024
WBLOCKS = D // WCOLS


def combine_body(parts, query, mask, weight, out, held, attended, sems):
    def fetch(b):
        return pltpu.make_async_copy(
            weight.at[:, b * WCOLS : (b + 1) * WCOLS], held.at[b], sems.at[b]
        )

    for b in range(WBLOCKS):
        fetch(b).start()
    lses = []
    for t in range(N_TENSOR):
        rows = parts[t, LSE_AT : LSE_AT + 16, :].astype(f32)
        lses.append(rows[0:4] + rows[4:8] + rows[8:12])
    for r in range(REQS):
        own = jnp.concatenate(
            [
                query[r * NODES : (r + 1) * NODES, h * HD : (h + 1) * HD]
                for h in range(HEADS)
            ],
            axis=0,
        )
        tree_keys = jnp.concatenate(
            [parts[4 * r + k, TREE_AT : TREE_AT + 8, :] for k in range(4)], axis=0
        )
        tree_values = jnp.concatenate(
            [parts[4 * r + k, TREE_AT + 8 : TREE_AT + 16, :] for k in range(4)], axis=0
        )
        allowed = mask[r] > 0
        scores = dot(tree_keys, own, ((1,), (1,))) * SCALE
        scores = jnp.where(allowed, scores, masked_score)
        overall = jnp.max(scores, axis=0, keepdims=True)
        for t in range(N_TENSOR):
            overall = jnp.maximum(overall, lses[t][r : r + 1])
        tree_weights = jnp.where(allowed, jnp.exp2(scores - overall), 0.0)
        denominator = jnp.sum(tree_weights, axis=0, keepdims=True)
        numerator = dot(tree_values, tree_weights.astype(bf16), ((0,), (0,)))
        for t in range(N_TENSOR):
            share = jnp.exp2(lses[t][r : r + 1] - overall)
            denominator = denominator + share
            numerator = numerator + share * parts[t, r * HD : (r + 1) * HD, :].astype(f32)
        mixed = (numerator * (1.0 / denominator)).T.astype(bf16)
        for h in range(HEADS):
            attended[r * NODES : (r + 1) * NODES, h * HD : (h + 1) * HD] = mixed[
                h * NODES : (h + 1) * NODES
            ]
    for b in range(WBLOCKS):
        fetch(b).wait()
        product = dot(attended[...], held[b], ((1,), (0,))).astype(bf16)
        out[2 * b] = product[:, :QCOLS]
        out[2 * b + 1] = product[:, QCOLS:]


def combine_project(parts, query, mask, weight):
    vmem = pl.BlockSpec(memory_space=pltpu.VMEM)
    return pl.pallas_call(
        combine_body,
        in_specs=[vmem, vmem, vmem, pl.BlockSpec(memory_space=pl.ANY)],
        out_specs=vmem,
        out_shape=jax.ShapeDtypeStruct((N_TENSOR, ROWS, QCOLS), bf16),
        scratch_shapes=[
            pltpu.VMEM((WBLOCKS, QCOLS, WCOLS), bf16),
            pltpu.VMEM((ROWS, QCOLS), bf16),
            pltpu.SemaphoreType.DMA((WBLOCKS,)),
        ],
        cost_estimate=pl.CostEstimate(
            flops=1_100_000_000, bytes_accessed=13_000_000, transcendentals=40_000
        ),
        name="combine_project",
    )(parts, query, mask, weight)


def draft_body(parts, residual, gain, chooser, weight, feature, out):
    total = residual[...].astype(f32)
    summed = parts[0].astype(f32)
    for t in range(1, N_TENSOR):
        summed = summed + parts[t].astype(f32)
    rounded = (total + summed).astype(bf16)
    feature[...] = rounded
    wide = rounded.astype(f32)
    squares = jnp.sum(wide * wide, axis=1, keepdims=True)
    eye = lax.broadcasted_iota(jnp.int32, (ROWS, ROWS), 0) == lax.broadcasted_iota(
        jnp.int32, (ROWS, ROWS), 1
    )
    squares_row = jnp.sum(jnp.where(eye, squares, 0.0), axis=0, keepdims=True)
    hi, mid, lo = split3(squares_row)
    pieces = jnp.concatenate(
        [hi.astype(f32), mid.astype(f32), lo.astype(f32), jnp.zeros((5, ROWS), f32)], axis=0
    ).astype(bf16)
    gained = (wide * gain[...].astype(f32)).astype(bf16)
    chosen = dot(chooser[...], gained, ((1,), (0,))).astype(bf16)
    product = dot(chosen, weight[...], ((1,), (0,))).astype(bf16)
    for t in range(N_TENSOR):
        out[t, 0:ROWS, :] = product[:, t * HD : (t + 1) * HD]
        out[t, ROWS : ROWS + 8, :] = pieces


def draft(parts, residual, gain, chooser, weight):
    vmem = pl.BlockSpec(memory_space=pltpu.VMEM)
    return pl.pallas_call(
        draft_body,
        in_specs=[vmem] * 5,
        out_specs=[vmem, vmem],
        out_shape=[
            jax.ShapeDtypeStruct((ROWS, QCOLS), bf16),
            jax.ShapeDtypeStruct((N_TENSOR, ROWS + 8, HD), bf16),
        ],
        cost_estimate=pl.CostEstimate(
            flops=300_000_000, bytes_accessed=5_000_000, transcendentals=0
        ),
        name="draft",
    )(parts, residual, gain, chooser, weight)


def finish_body(parts, chooser, out):
    summed = parts[0].astype(f32)
    for t in range(1, N_TENSOR):
        summed = summed + parts[t].astype(f32)
    squares = summed[ROWS : ROWS + 1] + summed[ROWS + 1 : ROWS + 2] + summed[ROWS + 2 : ROWS + 3]
    inverse = lax.rsqrt(squares / D + epsilon)
    column = jnp.sum(chooser[...].astype(f32) * inverse, axis=1, keepdims=True)
    out[...] = (summed[0:ROWS] * column).astype(bf16)


def finish(parts, chooser):
    vmem = pl.BlockSpec(memory_space=pltpu.VMEM)
    return pl.pallas_call(
        finish_body,
        in_specs=[vmem, vmem],
        out_specs=vmem,
        out_shape=jax.ShapeDtypeStruct((ROWS, HD), bf16),
        cost_estimate=pl.CostEstimate(flops=1_000_000, bytes_accessed=700_000, transcendentals=128),
        name="finish",
    )(parts, chooser)


def exchange(x):
    return lax.all_to_all(x, "tensor", 0, 0)


def shards(
    queries,
    tree_states,
    cache_codes,
    cache_scales,
    bit_widths,
    page_table,
    lengths,
    parents,
    tree_mask,
    output_weight,
    residual,
    norm_gain,
    draft_weight,
):
    place = lax.axis_index("tensor").astype(jnp.int32).reshape(1)
    every_query = exchange(jnp.broadcast_to(queries[None], (N_TENSOR, ROWS, QCOLS)))
    keys, values = dequantize(cache_codes, cache_scales, bit_widths, page_table, place)
    mask = jnp.tile(tree_mask.transpose(0, 2, 1), (1, 1, HEADS)).astype(f32)
    row_ids = (jnp.arange(REQS, dtype=jnp.int32)[:, None] * NODES + parents).reshape(ROWS)
    chooser = (row_ids[:, None] == jnp.arange(ROWS, dtype=jnp.int32)[None, :]).astype(bf16)
    parts = exchange(block_partial(place, lengths, every_query, keys, values, tree_states))
    products = exchange(combine_project(parts, queries, mask, output_weight))
    feature, drafted = draft(products, residual, norm_gain[None, :], chooser, draft_weight)
    return (feature, finish(exchange(drafted), chooser))


def solution(mesh):
    placed = (
        P("dp", "tensor"),
        P(("dp", "tensor"), None),
        P(("dp", "tensor"), None, None, None, None),
        P(("dp", "tensor"), None, None, None),
        P("dp"),
        P("dp", None),
        P("dp"),
        P("dp", None),
        P("dp", None, None),
        P("tensor", None),
        P("dp", "tensor"),
        P("tensor"),
        P("tensor", None),
    )
    return jax.shard_map(
        shards,
        mesh=mesh,
        in_specs=placed,
        out_specs=(P("dp", "tensor"), P("dp", "tensor")),
        check_vma=False,
    )
```

time: 532 us -> 153 us (0.29)
  blocking collectives: 193 us -> 15.9 us
  waiting for transfers between devices: 215 us -> 69.3 us
  local copies, waits for them, and re-layouts: 46.4 us -> 8.12 us
  Pallas kernels: 0 us -> 35 us
  other arithmetic: 26.4 us -> 0.77 us
  matrix products: 24 us -> 0 us
  starting transfers between devices: 0.16 us -> 21.4 us
  between operations: 14.7 us -> 0.7 us
  loops' own time: 11.5 us -> 0 us
    reduce_scatter x3 -> x0, waiting for transfers between devices: 165 us -> none  [the longest x1 84.9 us: shards(): lax.psum_scatter(jnp.dot(attended, output_weight, preferred_element_type=...]
    all_to_all x0 -> x3, waiting for transfers between devices: none -> 69.3 us  [exchange(): return lax.all_to_all(x, 'tensor', 0, 0)]
    pmax x1 -> x0, blocking collectives: 66.4 us -> none  [shards(): row_max = lax.pmax(maxima, 'tensor')]
    unnamed x1 -> x0, blocking collectives: 65.4 us -> none
    all_gather x1 -> x0, waiting for transfers between devices: 48.9 us -> none  [shards(): lax.all_gather(queries, 'tensor', axis=1, tiled=True)]
    pallas_call x0 -> x5, Pallas kernels: none -> 35 us  [the longest x1 15.2 us: block_partial(): pl.pallas_call(block_body, grid_spec=pltpu.PrefetchScalarGridSpec(num_sca...]
    psum x1 -> x0, blocking collectives: 33.3 us -> none  [shards(): lax.psum(jnp.sum(jnp.square(feature.astype(jnp.float32)), axis=1), 'tensor')]
    all_gather x1 -> x0, blocking collectives: 28 us -> none  [shards(): lax.all_gather(tree_states, 'tensor', axis=0, tiled=True)]
  transfers between devices with their start and end apart: 4 -> 3, of which waited for: 3 -> 3; matrix products, arithmetic and copies ran while one was open for 2% -> 2% of each run, Pallas kernels for 0% -> 5%
where the time goes in v1:
time: 153 us; the launch traced here: 151 us
  waiting for transfers between devices  69.3 us (45%)
  Pallas kernels  35 us (23%)
  starting transfers between devices  21.4 us (14%)
  blocking collectives  15.9 us (10%)
  local copies, waits for them, and re-layouts  8.12 us (5%)
    all_to_all x3, waiting for transfers between devices, exchange(): return lax.all_to_all(x, 'tensor', 0, 0)  69.3 us
    all_to_all x3, starting transfers between devices, exchange(): return lax.all_to_all(x, 'tensor', 0, 0)  21.4 us
    all_to_all x1, blocking collectives, exchange(): return lax.all_to_all(x, 'tensor', 0, 0)  15.9 us
    pallas_call x1, Pallas kernels, block_partial(): pl.pallas_call(block_body, grid_spec=pltpu.PrefetchScalarGridSpec(num_sca...  15.2 us
    pallas_call x1, Pallas kernels, dequantize(): pl.pallas_call(dequant_body, grid_spec=pltpu.PrefetchScalarGridSpec(num_s...  7.18 us
    pallas_call x1, Pallas kernels, combine_project(): pl.pallas_call(combine_body, in_specs=[vmem, vmem, vmem, pl.BlockSpec(mem...  6.87 us
    unnamed x12, local copies, waits for them, and re-layouts  4.11 us
    pallas_call x1, Pallas kernels, draft(): pl.pallas_call(draft_body, in_specs=[vmem] * 5, out_specs=[vmem, vmem], o...  3.98 us
  transfers between devices with their start and end apart: 3, of which 3 were waited for; matrix products, arithmetic and copies ran while one was open for 2% of the time, Pallas kernels for 5%

profile of v1, /device:TPU:2, one launch (start us, length us, event | category | flops | bytes accessed | tf_op | source)
XLA Modules:
  0.0 151.3 jit_solution(8192726441390746864)
XLA Ops:
  0.6 2.4 %broadcast_in_dim.4 = bf16[16,128,512]{2,1,0:T(8,128)(2,1)} broadcast(bf16[128,512]{1,0:T(8,128)(2,1)} %query.1), dimensions={1,2} | broadcast | bytes 2228224 | tf_op jit(solution)/shard_map/broadcast_in_dim | solution.py:326
  3.1 7.5 %all-to-all-start = ((bf16[16,128,512]{2,1,0:T(8,128)(2,1)}), bf16[16,128,512]{2,1,0:T(8,128)(2,1)S(1)}, u32[]{:S(2)}, u32[]{:S(2)}) async-start(bf16[16,128,512]{2,1,0:T(8,128)(2,1)} %broadcast_in_dim.4), calls=%async_computation | async-start | bytes 4194304 | tf_op jit(solution)/shard_map/all_to_all | solution.py:307
  10.5 7.2 %dequantize.1 = (bf16[4,8,320,128]{3,2,1,0:T(8,128)(2,1)}, bf16[4,8,128,320]{3,2,1,0:T(8,128)(2,1)}) custom-call(s32[4,80]{1,0:T(4,128)} %table.1, s32[1]{0:T(128)} %bitcast.place, s32[8]{0:T(128)} %bits.1, bf16[20,8,2,64,128]{4,3,2,1,0:T(8,128)(2,1)} %refs_4_.1, bf16[20,8,2,64,128]{4,3,2,1,0:T(8,128)(2,1)} %refs_4_.1, bf16[20,8,2,64,128]{4,3,2,1,0:T(8,128)(2,1)} %refs_4_.1, ...), custom_call_target="tpu_custom_call" | custom-call | flops 20000000 | bytes 10485760 | tf_op jit(solution)/shard_map/dequantize/pallas_call | solution.py:81
  17.7 20.0 %all-to-all-done.queries = bf16[16,128,512]{2,1,0:T(8,128)(2,1)S(1)} async-done(((bf16[16,128,512]{2,1,0:T(8,128)(2,1)}), bf16[16,128,512]{2,1,0:T(8,128)(2,1)S(1)}, u32[]{:S(2)}, u32[]{:S(2)}) %all-to-all-start) | async-done | bytes 2097184 | tf_op jit(solution)/shard_map/all_to_all | solution.py:307
  37.7 1.4 copy-done.2
  39.1 15.2 %block_partial.1 = bf16[16,544,128]{2,1,0:T(8,128)(2,1)} custom-call(s32[1]{0:T(128)} %bitcast.place, s32[4]{0:T(128)} %lengths.1, bf16[16,128,512]{2,1,0:T(8,128)(2,1)} %copy-done.2, bf16[4,8,320,128]{3,2,1,0:T(8,128)(2,1)} %get-tuple-element.6.keys, bf16[4,8,128,320]{3,2,1,0:T(8,128)(2,1)} %get-tuple-element.7.values, bf16[8,2048]{1,0:T(8,128)(2,1)} %tree.1), custom_call_target="tpu_custom_call" | custom-call | flops 1400000000 | bytes 10000000 | tf_op jit(solution)/shard_map/block_partial/pallas_call | solution.py:146
  54.3 7.0 %all-to-all-start.1 = ((bf16[16,544,128]{2,1,0:T(8,128)(2,1)}), bf16[16,544,128]{2,1,0:T(8,128)(2,1)S(1)}, u32[]{:S(2)}, u32[]{:S(2)}) async-start(bf16[16,544,128]{2,1,0:T(8,128)(2,1)} %block_partial.1), calls=%async_computation.1 | async-start | bytes 4456448 | tf_op jit(solution)/shard_map/all_to_all | solution.py:307
  61.3 0.1 copy.15
  61.5 0.8 convert_element_type.12.mask
  62.2 25.6 %all-to-all-done.1.parts = bf16[16,544,128]{2,1,0:T(8,128)(2,1)S(1)} async-done(((bf16[16,544,128]{2,1,0:T(8,128)(2,1)}), bf16[16,544,128]{2,1,0:T(8,128)(2,1)S(1)}, u32[]{:S(2)}, u32[]{:S(2)}) %all-to-all-start.1) | async-done | bytes 2228256 | tf_op jit(solution)/shard_map/all_to_all | solution.py:307
  87.9 1.4 copy-done
  89.2 6.9 %combine_project.1 = bf16[16,128,512]{2,1,0:T(8,128)(2,1)} custom-call(bf16[16,544,128]{2,1,0:T(8,128)(2,1)} %copy-done, bf16[128,512]{1,0:T(8,128)(2,1)} %query.1, f32[4,32,128]{2,1,0:T(8,128)} %convert_element_type.12.mask, bf16[512,8192]{1,0:T(8,128)(2,1)} %weight.2), custom_call_target="tpu_custom_call" | custom-call | flops 1100000000 | bytes 13000000 | tf_op jit(solution)/shard_map/combine_project/pallas_call | solution.py:225
  96.1 0.0 copy-start.4
  96.1 0.0 copy-start.5
  96.2 6.9 %all-to-all-start.2 = ((bf16[16,128,512]{2,1,0:T(8,128)(2,1)}), bf16[16,128,512]{2,1,0:T(8,128)(2,1)S(1)}, u32[]{:S(2)}, u32[]{:S(2)}) async-start(bf16[16,128,512]{2,1,0:T(8,128)(2,1)} %combine_project.1), calls=%async_computation.2 | async-start | bytes 4194304 | tf_op jit(solution)/shard_map/all_to_all | solution.py:307
  103.0 0.1 broadcast_add_fusion
  103.1 0.1 eq.15
  103.2 0.6 broadcast_in_dim.5.gain
  103.8 0.7 fusion.chooser
  104.5 23.7 %all-to-all-done.2.parts = bf16[16,128,512]{2,1,0:T(8,128)(2,1)S(1)} async-done(((bf16[16,128,512]{2,1,0:T(8,128)(2,1)}), bf16[16,128,512]{2,1,0:T(8,128)(2,1)S(1)}, u32[]{:S(2)}, u32[]{:S(2)}) %all-to-all-start.2) | async-done | bytes 2097184 | tf_op jit(solution)/shard_map/all_to_all | solution.py:307
  128.2 1.3 copy-done.1
  129.6 4.0 %draft.1 = (bf16[128,512]{1,0:T(8,128)(2,1)}, bf16[16,136,128]{2,1,0:T(8,128)(2,1)}) custom-call(bf16[16,128,512]{2,1,0:T(8,128)(2,1)} %copy-done.1, bf16[128,512]{1,0:T(8,128)(2,1)} %residual.1, bf16[1,512]{1,0:T(2,128)(2,1)} %broadcast_in_dim.5.gain, bf16[128,128]{1,0:T(8,128)(2,1)} %fusion.chooser, bf16[512,2048]{1,0:T(8,128)(2,1)} %weight.3), custom_call_target="tpu_custom_call" | custom-call | flops 300000000 | bytes 5000000 | tf_op jit(solution)/shard_map/draft/pallas_call | solution.py:269
  133.5 15.9 %all_to_all.20.parts = bf16[16,136,128]{2,1,0:T(8,128)(2,1)} all-to-all(bf16[16,136,128]{2,1,0:T(8,128)(2,1)} %get-tuple-element.9), channel_id=1, replica_groups=mesh['dp'=16,'tensor'=16] {'tensor'}, dimensions={0} | all-to-all | bytes 1114112 | tf_op jit(solution)/shard_map/all_to_all | solution.py:307
  149.5 1.8 %finish.1 = bf16[128,128]{1,0:T(8,128)(2,1)} custom-call(bf16[16,136,128]{2,1,0:T(8,128)(2,1)} %all_to_all.20.parts, bf16[128,128]{1,0:T(8,128)(2,1)} %fusion.chooser), custom_call_target="tpu_custom_call" | custom-call | flops 1000000 | bytes 700000 | tf_op jit(solution)/shard_map/finish/pallas_call | solution.py:296
  (10 shorter events, 0.1 us)
Async XLA Ops:
  3.1 34.6 %all-to-all-start = ((bf16[16,128,512]{2,1,0:T(8,128)(2,1)}), bf16[16,128,512]{2,1,0:T(8,128)(2,1)S(1)}, u32[]{:S(2)}, u32[]{:S(2)}) async-start(bf16[16,128,512]{2,1,0:T(8,128)(2,1)} %broadcast_in_dim.4), calls=%async_computation | async-start | bytes 4194304 | tf_op jit(solution)/shard_map/all_to_all | solution.py:307
  37.7 1.4 copy-start.2
  54.3 7.0 %copy-start.3 = (s32[4,32,32]{2,1,0:T(8,128)S(1)}, s32[4,32,32]{2,1,0:T(8,128)}, u32[]{:S(2)}) copy-start(s32[4,32,32]{2,1,0:T(8,128)} %param.21) | copy-start | bytes 49156
  54.3 33.6 %all-to-all-start.1 = ((bf16[16,544,128]{2,1,0:T(8,128)(2,1)}), bf16[16,544,128]{2,1,0:T(8,128)(2,1)S(1)}, u32[]{:S(2)}, u32[]{:S(2)}) async-start(bf16[16,544,128]{2,1,0:T(8,128)(2,1)} %block_partial.1), calls=%async_computation.1 | async-start | bytes 4456448 | tf_op jit(solution)/shard_map/all_to_all | solution.py:307
  87.9 1.4 copy-start
  96.1 6.9 %copy-start.4 = (s32[4,32]{1,0:T(4,128)S(1)}, s32[4,32]{1,0:T(4,128)}, u32[]{:S(2)}) copy-start(s32[4,32]{1,0:T(4,128)} %param.20) | copy-start | bytes 1540
  96.1 7.1 %copy-start.5 = (bf16[512]{0:T(512)(128)(2,1)S(1)}, bf16[512]{0:T(512)(128)(2,1)}, u32[]{:S(2)}) copy-start(bf16[512]{0:T(512)(128)(2,1)} %param.24) | copy-start | bytes 3076
  96.2 32.1 %all-to-all-start.2 = ((bf16[16,128,512]{2,1,0:T(8,128)(2,1)}), bf16[16,128,512]{2,1,0:T(8,128)(2,1)S(1)}, u32[]{:S(2)}, u32[]{:S(2)}) async-start(bf16[16,128,512]{2,1,0:T(8,128)(2,1)} %combine_project.1), calls=%async_computation.2 | async-start | bytes 4194304 | tf_op jit(solution)/shard_map/all_to_all | solution.py:307
  128.2 1.3 copy-start.1
